TPU v7x, 32 devices: a whole 2x2x4 slice. The times are simulated.
32 devices in a mesh: section: 2 (over x), dp: 16 (over z, y, core).
Axes of the slice: x: 2, y: 2, z: 4, core: 2. Of those that a mesh axis runs over, the one named last changes fastest.
Arguments:
- tokens_in: bfloat16 [3, 1024, 1024], P(None, 'dp'), may hold values from -6 to 6
- out_cotangent: bfloat16 [3, 1024, 1024], P(None, 'dp'), may hold values from -6 to 6
- in_weight: bfloat16 [2, 1024, 4384], P('section', 'dp'), may hold values from -0.1875 to 0.1875
- out_weight: bfloat16 [2, 2048, 1024], P('section', 'dp'), may hold values from -0.125 to 0.125
- norm_gain: float32 [2, 1024], P('section'), may hold values from 0.5 to 1.5
- conv_weight: float32 [2, 4, 2304], P('section'), may hold values from -3 to 3
- conv_bias: float32 [2, 2304], P('section'), may hold values from -3 to 3
- dt_bias: float32 [2, 32], P('section'), may hold values from -4 to 0
- a_log: float32 [2, 32], P('section'), may hold values from 0 to 2.77
- skip_gain: float32 [2, 32], P('section'), may hold values from 0.5 to 1.5
- gate_gain: float32 [2, 2048], P('section'), may hold values from 0.5 to 1.5
- group_fill: int32 [3, 32], P(None, 'dp'), may hold values from 0 to 32, as said below
- group_link: int32 [3, 32], P(None, 'dp'), may hold values from 0 to 1, as said below
Outputs:
- section_outputs: float32 [2, 3, 1024, 1024], P('section', None, 'dp')
- section_input_grads: float32 [2, 3, 1024, 1024], P('section', None, 'dp')
- grad_in_weight: float32 [2, 1024, 4384], P('section', 'dp')
- grad_out_weight: float32 [2, 2048, 1024], P('section', 'dp')
- grad_norm_gain: float32 [2, 1024], P('section')
- grad_conv_weight: float32 [2, 4, 2304], P('section')
- grad_conv_bias: float32 [2, 2304], P('section')
- grad_dt_bias: float32 [2, 32], P('section')
- grad_a_log: float32 [2, 32], P('section')
- grad_skip_gain: float32 [2, 32], P('section')
- grad_gate_gain: float32 [2, 2048], P('section')
Inputs may be any that keep to these rules, and one draw needn't show every extreme that they name: `group_fill`: each slot's groups hold whole sequences from the start of a group: a sequence fills groups, the last one from its start to its end, the rest of that group is unused; some groups are empty, and how many differs from slot to slot. Some group of every micro-batch is full. `group_link`: A link of 1 stands only on a group that is not the first of its slot, follows a full group and holds a token; every micro-batch has one.
All inputs are finite; a program needn't handle non-finite values.
Results may differ from a plain program's by a relative error of at most 0.0097.
Values may be sent and summed in bfloat16 or wider, within the bound.
No kernel may reach another device: no remote copies, remote signals or barrier semaphores. Data moves between devices by JAX's collectives and lax.ppermute only.
A program may use at most 128 MiB of HBM per device.

v0:
```python
import jax
import jax.numpy as jnp
from jax import lax
from jax.sharding import PartitionSpec as P

EPSILON = 1e-05
HIGHEST = lax.Precision.HIGHEST


def shifted_2(x, axis, by):
    peers = lax.axis_size(axis)
    pairs = [(i, i + by) for i in range(peers) if 0 <= i + by < peers]
    return lax.ppermute(x, axis, pairs)


def norm_map(values, gain_row):
    return (
        values * lax.rsqrt(jnp.mean(values * values, axis=-1, keepdims=True) + EPSILON) * gain_row
    )


def ssd_scan(x_heads, step_size, log_decay, input_b, input_c, link_row, groups):
    rows_all, head_count, head_size = x_heads.shape
    length = rows_all // groups
    state_size = input_b.shape[1]
    x_blocks = x_heads.reshape(groups, length, head_count, head_size)
    dt_blocks = step_size.reshape(groups, length, head_count)
    cumulative = jnp.cumsum(log_decay.reshape(groups, length, head_count), axis=1)
    b_blocks = input_b.reshape(groups, length, state_size)
    c_blocks = input_c.reshape(groups, length, state_size)
    scores = jnp.einsum("cin,cjn->cij", c_blocks, b_blocks, precision=HIGHEST)
    causal = jnp.arange(length)[:, None] >= jnp.arange(length)[None, :]
    decay_gap = cumulative[:, :, None, :] - cumulative[:, None, :, :]
    factors = jnp.exp(jnp.where(causal[None, :, :, None], decay_gap, -jnp.inf))
    factors = factors * scores[..., None] * dt_blocks[:, None, :, :]
    diag_out = jnp.einsum("cijh,cjhp->cihp", factors, x_blocks, precision=HIGHEST)
    group_end = cumulative[:, -1:, :]
    to_end = jnp.exp(group_end - cumulative) * dt_blocks
    group_states = jnp.einsum("cjh,cjhp,cjn->chpn", to_end, x_blocks, b_blocks, precision=HIGHEST)
    group_decay = jnp.exp(group_end[:, 0, :])
    link_float = link_row.astype(jnp.float32)
    carried = jnp.zeros((head_count, head_size, state_size), jnp.float32)
    entering = [carried]
    carried = link_float[1] * (group_decay[0][:, None, None] * carried + group_states[0])
    entering.append(carried)
    entering = jnp.stack(entering)
    off_out = jnp.einsum(
        "cih,cin,chpn->cihp", jnp.exp(cumulative), c_blocks, entering, precision=HIGHEST
    )
    return (diag_out + off_out).reshape(rows_all, head_count, head_size)


def mixer_slot(
    projected, conv_weight, conv_bias, dt_bias, a_log, skip_gain, gate_gain, fill_row, link_row
):
    rows_all = projected.shape[0]
    groups = fill_row.shape[0]
    length = rows_all // groups
    inner_size = gate_gain.shape[0]
    head_count = dt_bias.shape[0]
    conv_size = conv_bias.shape[0]
    state_size = (conv_size - inner_size) // 2
    head_size = inner_size // head_count
    gate_part = projected[:, :inner_size]
    conv_in = projected[:, inner_size : inner_size + conv_size]
    dt_raw = projected[:, inner_size + conv_size :]
    within = jnp.arange(rows_all) % length
    linked = jnp.broadcast_to(link_row.astype(jnp.float32)[:, None], (groups, length)).reshape(
        rows_all
    )
    filled = jnp.broadcast_to(fill_row[:, None], (groups, length)).reshape(rows_all)
    valid = (within < filled).astype(jnp.float32)
    conv_sum = conv_bias + conv_weight[0] * conv_in
    for lag_steps in range(1, conv_weight.shape[0]):
        shifted = jnp.concatenate(
            [jnp.zeros((lag_steps, conv_size), jnp.float32), conv_in[:-lag_steps]], axis=0
        )
        keep_mask = jnp.maximum((within >= lag_steps).astype(jnp.float32), linked)
        conv_sum = conv_sum + conv_weight[lag_steps] * shifted * keep_mask[:, None]
    activated = jax.nn.silu(conv_sum)
    x_heads = activated[:, :inner_size].reshape(rows_all, head_count, head_size)
    input_b = activated[:, inner_size : inner_size + state_size]
    input_c = activated[:, inner_size + state_size :]
    step_size = jax.nn.softplus(dt_raw + dt_bias)
    log_decay = step_size * -jnp.exp(a_log)
    scanned = ssd_scan(x_heads, step_size, log_decay, input_b, input_c, link_row, groups)
    scanned = scanned + skip_gain[:, None] * x_heads
    gated = scanned.reshape(rows_all, inner_size) * jax.nn.silu(gate_part)
    return norm_map(gated, gate_gain) * valid[:, None]


def outer_term(left_rows, right_rows):
    return lax.dot_general(
        left_rows, right_rows, (((0,), (0,)), ((), ())), preferred_element_type=jnp.float32
    )


def on_device(
    tokens_in,
    out_cotangent,
    in_weight,
    out_weight,
    norm_gain,
    conv_weight,
    conv_bias,
    dt_bias,
    a_log,
    skip_gain,
    gate_gain,
    group_fill,
    group_link,
):
    contract_cols = (((1,), (1,)), ((), ()))
    micro_count = tokens_in.shape[0]
    section_count = lax.axis_size("section")
    section_index = lax.axis_index("section")
    is_first = section_index == 0
    is_last = section_index == section_count - 1
    tick_count = micro_count + section_count - 1
    params = (conv_weight[0], conv_bias[0], dt_bias[0], a_log[0], skip_gain[0], gate_gain[0])
    gain_row = norm_gain[0]
    full_in, full_out = (
        lax.all_gather(in_weight, "dp", axis=1, tiled=True),
        lax.all_gather(out_weight, "dp", axis=1, tiled=True),
    )
    weight_in = full_in[0]
    weight_out = full_out[0]
    tick_list = jnp.arange(tick_count, dtype=jnp.int32)

    def forward_tick(received, tick_index):
        batch_index = jnp.clip(tick_index - section_index, 0, micro_count - 1)
        own_rows = lax.dynamic_index_in_dim(
            tokens_in, jnp.minimum(tick_index, micro_count - 1), 0, keepdims=False
        )
        layer_in = jnp.where(is_first, own_rows, received)
        fill_row = lax.dynamic_index_in_dim(group_fill, batch_index, 0, keepdims=False)
        link_row = lax.dynamic_index_in_dim(group_link, batch_index, 0, keepdims=False)
        residual = layer_in.astype(jnp.float32)
        normed = norm_map(residual, gain_row).astype(jnp.bfloat16)
        projected = jnp.dot(normed, weight_in, preferred_element_type=jnp.float32)
        mixed = mixer_slot(projected, *params, fill_row, link_row).astype(jnp.bfloat16)
        output = residual + jnp.dot(mixed, weight_out, preferred_element_type=jnp.float32)
        sent = shifted_2(output.astype(jnp.bfloat16), "section", 1)
        return (sent, (layer_in, normed, projected, mixed, output))

    start_rows = jnp.zeros(tokens_in.shape[1:], jnp.bfloat16)
    unused_rows, kept = lax.scan(forward_tick, start_rows, tick_list)
    stack_inputs, stack_normed, stack_projected, stack_mixed, stack_outputs = kept
    section_outputs = lax.dynamic_slice_in_dim(stack_outputs, section_index, micro_count, 0)[None]
    again_in, again_out = (
        lax.all_gather(in_weight, "dp", axis=1, tiled=True),
        lax.all_gather(out_weight, "dp", axis=1, tiled=True),
    )
    weight_in = again_in[0]
    weight_out = again_out[0]

    def backward_tick(carry, tick_index):
        back_received, small_sums, shard_in, shard_out = carry
        saved_index = jnp.clip(
            tick_index - section_count + 1 + 2 * section_index, 0, tick_count - 1
        )
        batch_index = jnp.clip(tick_index - section_count + 1 + section_index, 0, micro_count - 1)
        own_grad = lax.dynamic_index_in_dim(
            out_cotangent, jnp.minimum(tick_index, micro_count - 1), 0, keepdims=False
        ).astype(jnp.float32)
        own_grad = jnp.where(tick_index < micro_count, own_grad, jnp.zeros_like(own_grad))
        upstream = jnp.where(is_last, own_grad, back_received.astype(jnp.float32))
        fill_row = lax.dynamic_index_in_dim(group_fill, batch_index, 0, keepdims=False)
        link_row = lax.dynamic_index_in_dim(group_link, batch_index, 0, keepdims=False)
        residual = lax.dynamic_index_in_dim(stack_inputs, saved_index, 0, keepdims=False).astype(
            jnp.float32
        )
        normed = lax.dynamic_index_in_dim(stack_normed, saved_index, 0, keepdims=False)
        projected = lax.dynamic_index_in_dim(stack_projected, saved_index, 0, keepdims=False)
        mixed = lax.dynamic_index_in_dim(stack_mixed, saved_index, 0, keepdims=False)
        upper_lower = upstream.astype(jnp.bfloat16)
        d_mixed = lax.dot_general(
            upper_lower, weight_out, contract_cols, preferred_element_type=jnp.float32
        )

        def local_map(proj_rows, *param_list):
            return mixer_slot(proj_rows, *param_list, fill_row, link_row)

        unused, pull_back = jax.vjp(local_map, projected, *params)
        pulled = pull_back(d_mixed)
        d_low = pulled[0].astype(jnp.bfloat16)
        d_normed = lax.dot_general(
            d_low, weight_in, contract_cols, preferred_element_type=jnp.float32
        )
        unused_norm, pull_norm = jax.vjp(norm_map, residual, gain_row)
        d_residual, d_gain = pull_norm(d_normed)
        input_grad = upstream + d_residual
        tick_small = (d_gain,) + tuple(pulled[1:])
        small_sums = jax.tree.map(jnp.add, small_sums, tick_small)
        sent_back = shifted_2(input_grad.astype(jnp.bfloat16), "section", -1)
        return (
            (sent_back, small_sums, shard_in, shard_out),
            (normed, d_low, mixed, upper_lower, input_grad),
        )

    small_start = jax.tree.map(
        lambda item: jnp.zeros(item.shape, jnp.float32), (gain_row,) + params
    )
    shard_start_in = jnp.zeros(in_weight.shape[1:], jnp.float32)
    shard_start_out = jnp.zeros(out_weight.shape[1:], jnp.float32)
    carry_start = (start_rows, small_start, shard_start_in, shard_start_out)
    carry_end, tick_outputs = lax.scan(backward_tick, carry_start, tick_list)
    unused_back, small_sums, shard_in, shard_out = carry_end
    list_normed, list_dproj, list_mixed, list_uplow, list_grads = tick_outputs
    all_normed = list_normed.reshape(-1, list_normed.shape[-1])
    all_dproj = list_dproj.reshape(-1, list_dproj.shape[-1])
    all_mixed = list_mixed.reshape(-1, list_mixed.shape[-1])
    all_uplow = list_uplow.reshape(-1, list_uplow.shape[-1])
    shard_in = lax.psum_scatter(
        outer_term(all_normed, all_dproj), "dp", scatter_dimension=0, tiled=True
    )
    shard_out = lax.psum_scatter(
        outer_term(all_mixed, all_uplow), "dp", scatter_dimension=0, tiled=True
    )
    summed = lax.psum(small_sums, "dp")
    section_input_grads = lax.dynamic_slice_in_dim(
        list_grads, section_count - 1 - section_index, micro_count, 0
    )[None]
    return (section_outputs, section_input_grads, shard_in[None], shard_out[None]) + tuple(
        (summed_grad[None] for summed_grad in summed)
    )


def solution(mesh):
    in_specs = (
        P(None, "dp", None),
        P(None, "dp", None),
        P("section", "dp", None),
        P("section", "dp", None),
        P("section", None),
        P("section", None, None),
        P("section", None),
        P("section", None),
        P("section", None),
        P("section", None),
        P("section", None),
        P(None, "dp"),
        P(None, "dp"),
    )
    out_specs = (
        P("section", None, "dp", None),
        P("section", None, "dp", None),
        P("section", "dp", None),
        P("section", "dp", None),
        P("section", None),
        P("section", None, None),
        P("section", None),
        P("section", None),
        P("section", None),
        P("section", None),
        P("section", None),
    )
    return jax.shard_map(
        on_device, mesh=mesh, in_specs=in_specs, out_specs=out_specs, check_vma=False
    )
```

profile of v0, /device:TPU:0, one launch (start us, length us, event | category | flops | bytes accessed | tf_op | source)
XLA Modules:
  0.0 1077.1 jit_solution(11850100364788017831)
XLA Ops:
  12.7 50.6 %all-gather.5.cloned.1.call-done = bf16[1,2048,1024]{2,1,0:T(8,128)(2,1)} async-done(((bf16[1,128,1024]{2,1,0:T(8,128)(2,1)}), bf16[1,2048,1024]{2,1,0:T(8,128)(2,1)}) %all-gather.5.cloned.1.call-update) | async-done | bytes 4194320 | tf_op jit(solution)/shard_map/all_gather | solution.py:124
  63.3 80.1 %all-gather.3.cloned.1.call-done = bf16[1,1024,4384]{2,1,0:T(8,128)(2,1)} async-done(((bf16[1,64,4384]{2,1,0:T(8,128)(2,1)}), bf16[1,1024,4384]{2,1,0:T(8,128)(2,1)}) %all-gather.3.cloned.1.call-update) | async-done | bytes 8978448 | tf_op jit(solution)/shard_map/all_gather | solution.py:123
  147.9 184.0 %while.61 = (s32[]{:T(128)}, bf16[64,1024]{1,0:T(8,128)(2,1)S(1)}, bf16[4,64,1024]{2,1,0:T(8,128)(2,1)}, bf16[4,64,1024]{2,1,0:T(8,128)(2,1)}, f32[4,64,4384]{2,...) while((s32[]{:T(128)}, bf16[64,1024]{1,0:T(8,128)(2,1)S(1)}, ...), condition=%wide.region_4.5_spmd, body=%wide.region_0.4_spmd.sunk | while | flops 1205211648 | bytes 37663164 | solution.py:147
  153.6 6.4 bitcast_dynamic-update-slice_fusion.17
  199.3 6.4 bitcast_dynamic-update-slice_fusion.17
  232.8 4.4 collective-permute-start
  245.4 6.4 bitcast_dynamic-update-slice_fusion.17
  279.0 4.4 collective-permute-start
  291.5 6.4 bitcast_dynamic-update-slice_fusion.17
  325.0 4.4 collective-permute-start
  336.5 430.2 %while.62 = (s32[]{:T(128)}, bf16[64,1024]{1,0:T(8,128)(2,1)S(1)}, f32[1024]{0:T(1024)}, f32[4,2304]{1,0:T(4,128)}, f32[2304]{0:T(1024)}, /*index=5*/f32[32]{0:T...) while((s32[]{:T(128)}, bf16[64,1024]{1,0:T(8,128)(2,1)S(1)}, ...), condition=%wide.region_29.30_spmd.clone, body=%wide.region_5.29_spmd.clone.sunk | while | flops 1929479168 | bytes 110034496 | solution.py:207
  392.4 4.4 multiply_reduce_fusion.25
  405.0 4.1 fusion.300
  409.2 3.9 multiply_reduce_fusion.27
  444.0 6.7 fusion.305
  494.8 4.4 multiply_reduce_fusion.25
  507.3 4.1 fusion.300
  511.5 3.9 multiply_reduce_fusion.27
  546.3 6.7 fusion.305
  597.1 4.4 multiply_reduce_fusion.25
  609.7 4.1 fusion.300
  613.8 3.9 multiply_reduce_fusion.27
  648.6 6.7 fusion.305
  699.5 4.4 multiply_reduce_fusion.25
  712.0 4.1 fusion.300
  716.2 3.9 multiply_reduce_fusion.27
  751.0 6.7 fusion.305
  766.7 6.0 convolution_bitcast_fusion.6
  774.5 8.9 convolution_bitcast_fusion.5
  784.3 61.2 %all-reduce.24 = (f32[1,1024]{1,0:T(1,128)}, f32[1,4,2304]{2,1,0:T(4,128)}, f32[1,2304]{1,0:T(1,128)}, f32[1,32]{1,0:T(1,128)}, f32[1,32]{1,0:T(1,128)}, /*index=5*/f32[1,32]{1,0:T(1,128)}, f32[1,2048]{1,0:T(1,128)}) all-reduce(f32[1,1024]{1,0:T(1,128)S(1)} %bitcast.403, ...), channel_id=1, replica_groups=mesh['section'=2,'dp'=16] {'dp'}, use_global_device_ids=true, to_apply=%region_32.33 | all-reduce | flops 14688 | bytes 117504 | tf_op jit(solution)/shard_map/psum | solution.py:220
  846.8 29.4 %reduce-scatter.5.cloned.1.call-done = f32[128,1024]{1,0:T(8,128)} async-done(((f32[2048,1024]{1,0:T(8,128)}), f32[128,1024]{1,0:T(8,128)}) %reduce-scatter.5.cloned.1.call-update) | async-done | bytes 524304 | tf_op jit(solution)/shard_map/reduce_scatter | solution.py:217
  876.1 194.0 %reduce-scatter.3.cloned.1.call-done = f32[64,4384]{1,0:T(8,128)} async-done(((f32[1024,4384]{1,0:T(8,128)}), f32[64,4384]{1,0:T(8,128)}) %reduce-scatter.3.cloned.1.call-update) | async-done | bytes 1122320 | tf_op jit(solution)/shard_map/reduce_scatter | solution.py:214
  (1357 shorter events, 477.8 us)
Async XLA Ops:
  7.2 140.7 %copy-start.28 = (f32[1,2048]{1,0:T(1,128)S(1)}, f32[1,2048]{1,0:T(1,128)}, u32[]{:S(2)}) copy-start(f32[1,2048]{1,0:T(1,128)} %param.27) | copy-start | bytes 24580
  7.2 140.7 %copy-start.27 = (f32[1,1024]{1,0:T(1,128)S(1)}, f32[1,1024]{1,0:T(1,128)}, u32[]{:S(2)}) copy-start(f32[1,1024]{1,0:T(1,128)} %param.21) | copy-start | bytes 12292
  7.2 56.1 %all-gather.5.cloned.1.call-start = ((), (), s32[]{:S(2)}) async-start(), calls=%async_computation.3 | async-start | bytes 4456448 | tf_op jit(solution)/shard_map/all_gather | solution.py:124
  7.9 135.4 %all-gather.3.cloned.1.call-start = ((), (), s32[]{:S(2)}) async-start(), calls=%async_computation.2 | async-start | bytes 9748480 | tf_op jit(solution)/shard_map/all_gather | solution.py:123
  8.7 867.4 %reduce-scatter.5.cloned.1.call-start = ((), (), s32[]{:S(2)}) async-start(), calls=%async_computation.5 | async-start | bytes 8912896 | tf_op jit(solution)/shard_map/reduce_scatter | solution.py:217
  187.1 6.5 collective-permute-start
  232.8 6.9 collective-permute-start
  279.0 6.9 collective-permute-start
  325.0 6.9 collective-permute-start
  357.2 35.3 %copy-start.12 = (bf16[64,1024]{1,0:T(8,128)(2,1)}, bf16[64,1024]{1,0:T(8,128)(2,1)S(1)}, u32[]{:S(2)}) copy-start(bf16[64,1024]{1,0:T(8,128)(2,1)S(1)} %get-tuple-element.2087) | copy-start | bytes 393220 | tf_op jit(solution)/shard_map/while
  443.9 10.1 copy-start.55
  444.0 10.2 copy-start.58
  452.5 6.8 collective-permute-start.1
  459.5 35.3 %copy-start.12 = (bf16[64,1024]{1,0:T(8,128)(2,1)}, bf16[64,1024]{1,0:T(8,128)(2,1)S(1)}, u32[]{:S(2)}) copy-start(bf16[64,1024]{1,0:T(8,128)(2,1)S(1)} %get-tuple-element.2087) | copy-start | bytes 393220 | tf_op jit(solution)/shard_map/while
  546.2 10.1 copy-start.54
  546.3 10.1 copy-start.56
  546.3 10.2 copy-start.55
  546.3 10.2 copy-start.58
  554.9 6.8 collective-permute-start.1
  561.8 35.3 %copy-start.12 = (bf16[64,1024]{1,0:T(8,128)(2,1)}, bf16[64,1024]{1,0:T(8,128)(2,1)S(1)}, u32[]{:S(2)}) copy-start(bf16[64,1024]{1,0:T(8,128)(2,1)S(1)} %get-tuple-element.2087) | copy-start | bytes 393220 | tf_op jit(solution)/shard_map/while
  648.6 10.1 copy-start.54
  648.6 10.1 copy-start.56
  648.6 10.2 copy-start.55
  648.6 10.2 copy-start.58
  657.2 6.8 collective-permute-start.1
  664.2 35.3 %copy-start.12 = (bf16[64,1024]{1,0:T(8,128)(2,1)}, bf16[64,1024]{1,0:T(8,128)(2,1)S(1)}, u32[]{:S(2)}) copy-start(bf16[64,1024]{1,0:T(8,128)(2,1)S(1)} %get-tuple-element.2087) | copy-start | bytes 393220 | tf_op jit(solution)/shard_map/while
  751.0 10.1 copy-start.55
  751.0 10.2 copy-start.58
  759.6 6.8 collective-permute-start.1
  772.7 297.4 %reduce-scatter.3.cloned.1.call-start = ((), (), s32[]{:S(2)}) async-start(), calls=%async_computation.4 | async-start | bytes 19496960 | tf_op jit(solution)/shard_map/reduce_scatter | solution.py:214
  783.5 62.0 %copy-start.43 = (f32[4,64,1024]{2,1,0:T(8,128)S(1)}, f32[4,64,1024]{2,1,0:T(8,128)}, u32[]{:S(2)}) copy-start(f32[4,64,1024]{2,1,0:T(8,128)} %get-tuple-element.969) | copy-start | bytes 3145732
  783.5 62.0 %copy-start.44 = (f32[4,64,1024]{2,1,0:T(8,128)S(1)}, f32[4,64,1024]{2,1,0:T(8,128)}, u32[]{:S(2)}) copy-start(f32[4,64,1024]{2,1,0:T(8,128)} %get-tuple-element.964) | copy-start | bytes 3145732
  (357 other events, 1691.6 us)
Sparse Core Ops, SparseCore 0:
  10.2 53.0 all-gather.4
  65.6 77.7 all-gather.2
  772.9 103.2 reduce-scatter.4
  880.8 189.3 reduce-scatter.2
where the time goes:
time: 1090 us; the launch traced here: 1080 us
  waiting for transfers between devices  360 us (33%)
  matrix products  249 us (23%)
  local copies, waits for them, and re-layouts  170 us (16%)
  other arithmetic  161 us (15%)
  blocking collectives  61.2 us (6%)
  loops' own time  39.4 us (4%)
  starting transfers between devices  21.8 us (2%)
  between operations  14.3 us (1%)
    reduce_scatter x1, waiting for transfers between devices, on_device(): lax.psum_scatter(outer_term(all_normed, all_dproj), 'dp', scatter_dimensi...  194 us
    all_gather x1, waiting for transfers between devices, on_device(): lax.all_gather(in_weight, 'dp', axis=1, tiled=True)  80.1 us
    psum x1, blocking collectives, on_device(): summed = lax.psum(small_sums, 'dp')  61.2 us
    all_gather x1, waiting for transfers between devices, on_device(): lax.all_gather(out_weight, 'dp', axis=1, tiled=True)  50.6 us
    dot_general x16, matrix products, ssd_scan(): jnp.einsum('cijh,cjhp->cihp', factors, x_blocks, precision=HIGHEST)  48.8 us
    another operation x1, loops' own time, on_device(): carry_end, tick_outputs = lax.scan(backward_tick, carry_start, tick_list)  33.3 us
    dot_general x12, matrix products, ssd_scan(): jnp.einsum('cih,cin,chpn->cihp', jnp.exp(cumulative), c_blocks, entering,...  31.7 us
    reduce_scatter x1, waiting for transfers between devices, on_device(): lax.psum_scatter(outer_term(all_mixed, all_uplow), 'dp', scatter_dimensio...  29.4 us
  transfers between devices with their start and end apart: 12, of which 12 were waited for; matrix products, arithmetic and copies ran while one was open for 4% of the time, Pallas kernels for 0%

commit v1 on v0

v1 whole, which is shorter than its diff:
```python
import functools

import jax
import jax.numpy as jnp
from jax import lax
from jax.experimental import pallas as pl
from jax.experimental.pallas import tpu as pltpu
from jax.sharding import PartitionSpec as P

EPSILON = 1e-05
F32 = jnp.float32
BF16 = jnp.bfloat16
NN = (((1,), (0,)), ((), ()))
NT = (((1,), (1,)), ((), ()))
TN = (((0,), (0,)), ((), ()))
PACK = 4
VMEM_LIMIT = 56 * 1024 * 1024


def shifted_2(x, axis, by):
    peers = lax.axis_size(axis)
    pairs = [(i, i + by) for i in range(peers) if 0 <= i + by < peers]
    return lax.ppermute(x, axis, pairs)


def norm_map(values, gain_row):
    return (
        values * lax.rsqrt(jnp.mean(values * values, axis=-1, keepdims=True) + EPSILON) * gain_row
    )


def mm(left, right, dims):
    return lax.dot_general(left, right, dims, preferred_element_type=F32)


def split(values, parts):
    terms = []
    for _ in range(parts - 1):
        head = values.astype(BF16)
        terms.append(head)
        values = values - head.astype(F32)
    terms.append(values.astype(BF16))
    return terms


def mm3(left, right, dims):
    return (
        mm(left[0], right[0], dims) + mm(left[1], right[0], dims) + mm(left[0], right[1], dims)
    )


def mm_exact(left, right, dims, parts=3):
    if left.dtype == BF16:
        return sum(mm(left, term, dims) for term in split(right, parts))
    return sum(mm(term, right, dims) for term in split(left, parts))


def sigmoid(values):
    return 1.0 / (1.0 + jnp.exp(-values))


class Slot:
    def __init__(self, sizes, fill_ref, link_ref, proj_ref, cw_ref, cb_ref, dtb_ref, alog_ref, expand_ref):
        rows, groups, inner, conv, heads = sizes
        length = rows // groups
        width = rows * PACK
        self.rows, self.width = rows, width
        self.inner, self.conv, self.heads = inner, conv, heads
        self.proj_ref, self.cw_ref, self.cb_ref = proj_ref, cw_ref, cb_ref
        slot = pl.program_id(0)
        row = lax.broadcasted_iota(jnp.int32, (rows, width), 0)
        lane = lax.broadcasted_iota(jnp.int32, (rows, width), 1)
        lane_in = lane % rows
        row_seg = jnp.zeros((rows, width), jnp.int32)
        lane_seg = jnp.zeros((rows, width), jnp.int32)
        linked = jnp.zeros((rows, width), jnp.int32)
        filled = jnp.zeros((rows, width), jnp.int32)
        segment = jnp.int32(0)
        for group in range(groups):
            link = link_ref[slot, group]
            if group:
                segment = segment + (1 - link)
            row_here = (row // length) == group
            row_seg = jnp.where(row_here, segment, row_seg)
            lane_seg = jnp.where((lane_in // length) == group, segment, lane_seg)
            linked = jnp.where(row_here, link, linked)
            filled = jnp.where(row_here, fill_ref[slot, group], filled)
        within = row % length
        self.valid = (within < filled).astype(F32)
        self.keeps = [
            jnp.where(
                (row >= lag) & ((within >= lag) | (linked == 1)), 1.0, 0.0
            ).astype(F32)
            for lag in range(1, cw_ref.shape[0])
        ]
        same = row_seg == lane_seg
        self.causal = same & (lane_in <= row)
        self.anti = same & (lane_in >= row)
        self.eye = lane_in == row
        self.block = [(lane // rows == part).astype(F32).astype(BF16) for part in range(PACK)]
        low = lax.broadcasted_iota(jnp.int32, (rows, rows), 0)
        high = lax.broadcasted_iota(jnp.int32, (rows, rows), 1)
        self.tril = (low >= high).astype(F32).astype(BF16)
        self.triu = (low <= high).astype(F32).astype(BF16)
        self.bc_at = inner + inner
        self.bc_pre = self.conv_pre(inner, self.bc_at)
        bc = self.bc_pre * sigmoid(self.bc_pre)
        state = (conv - inner) // 2
        self.b_split = split(bc[:, :state], 2)
        self.c_split = split(bc[:, state:], 2)
        self.b_tall = [jnp.concatenate([term] * PACK, axis=0) for term in self.b_split]
        self.scores = mm3(self.c_split, self.b_tall, NT)
        self.dt_in = proj_ref[:, inner + conv :] + dtb_ref[...]
        self.step = jnp.maximum(self.dt_in, 0.0) + jnp.log1p(jnp.exp(-jnp.abs(self.dt_in)))
        self.rate = -jnp.exp(alog_ref[...])
        self.log_decay = self.step * self.rate
        cumulative = mm_exact(self.tril, self.log_decay, NN)
        self.spread = mm_exact(
            jnp.concatenate([cumulative, self.step], axis=0), expand_ref[...], NN
        )

    def conv_pre(self, at, proj_at):
        width = self.width
        conv_in = self.proj_ref[:, pl.ds(proj_at, width)]
        taps = self.cw_ref[:, pl.ds(at, width)]
        pre = self.cb_ref[:, pl.ds(at, width)] + taps[0:1] * conv_in
        for lag, keep in enumerate(self.keeps, 1):
            pre = pre + taps[lag : lag + 1] * (pltpu.roll(conv_in, lag, 0) * keep)
        return pre

    def diagonal(self, terms):
        return [
            jnp.concatenate([term * mask for mask in self.block], axis=0) for term in terms
        ]

    def decay(self, cum):
        across = jnp.sum(jnp.where(self.eye, cum, 0.0), axis=0, keepdims=True)
        return jnp.exp(jnp.where(self.causal, cum - across, -1e30)), across


def forward_kernel(
    sizes, fill_ref, link_ref, proj_ref, cw_ref, cb_ref, dtb_ref, alog_ref, skip_ref, gain_ref,
    expand_ref, mixed_ref, spread_ref, gated_ref,
):
    slot = Slot(sizes, fill_ref, link_ref, proj_ref, cw_ref, cb_ref, dtb_ref, alog_ref, expand_ref)
    rows, width, inner = slot.rows, slot.width, slot.inner
    spread_ref[...] = slot.spread
    steps = inner // width

    def one_pack(index, total):
        at = pl.multiple_of(index * width, width)
        here = pl.ds(at, width)
        pre = slot.conv_pre(at, pl.multiple_of(inner + at, width))
        xs = pre * sigmoid(pre)
        decay, _ = slot.decay(spread_ref[:rows, here])
        weights = split(slot.scores * decay, 2)
        scaled = slot.diagonal(split(xs * spread_ref[rows:, here], 2))
        scanned = mm3(weights, scaled, NN) + skip_ref[:, here] * xs
        gate = proj_ref[:, here]
        gated = scanned * (gate * sigmoid(gate))
        gated_ref[:, here] = gated
        return total + gated * gated

    total = lax.fori_loop(0, steps, one_pack, jnp.zeros((rows, width), F32))
    mean = jnp.sum(total, axis=1, keepdims=True) * (1.0 / inner)
    scale = slot.valid * lax.rsqrt(mean + EPSILON)

    def one_store(index, carry):
        here = pl.ds(pl.multiple_of(index * width, width), width)
        mixed_ref[:, here] = (gated_ref[:, here] * scale * gain_ref[:, here]).astype(BF16)
        return carry

    lax.fori_loop(0, steps, one_store, 0)


def backward_kernel(
    sizes, fill_ref, link_ref, proj_ref, dmix_ref, cw_ref, cb_ref, dtb_ref, alog_ref, skip_ref,
    gain_ref, expand_ref, collect_ref, dproj_ref, dcw_ref, dcb_ref, ddt_ref, dalog_ref, dskip_ref,
    dgain_ref, spread_ref, pre_ref, scan_ref, decay_ref,
):
    @pl.when(pl.program_id(0) == 0)
    def _():
        for ref in (dcw_ref, dcb_ref, ddt_ref, dalog_ref, dskip_ref, dgain_ref):
            ref[...] = jnp.zeros_like(ref)

    slot = Slot(sizes, fill_ref, link_ref, proj_ref, cw_ref, cb_ref, dtb_ref, alog_ref, expand_ref)
    rows, width, inner, conv = slot.rows, slot.width, slot.inner, slot.conv
    spread_ref[...] = slot.spread
    steps = inner // width
    c_tall = [jnp.concatenate([term] * PACK, axis=0) for term in slot.c_split]
    scores_back = mm3(slot.b_split, c_tall, NT)

    def first(index, totals):
        square, product = totals
        at = pl.multiple_of(index * width, width)
        here = pl.ds(at, width)
        pre = slot.conv_pre(at, pl.multiple_of(inner + at, width))
        pre_ref[:, here] = pre
        xs = pre * sigmoid(pre)
        decay, _ = slot.decay(spread_ref[:rows, here])
        decay_ref[:, here] = decay
        weights = split(slot.scores * decay, 2)
        scaled = slot.diagonal(split(xs * spread_ref[rows:, here], 2))
        scanned = mm3(weights, scaled, NN) + skip_ref[:, here] * xs
        scan_ref[:, here] = scanned
        gate = proj_ref[:, here]
        gated = scanned * (gate * sigmoid(gate))
        scaled_grad = dmix_ref[:, here] * slot.valid * gain_ref[:, here]
        return square + gated * gated, product + scaled_grad * gated

    zeros = jnp.zeros((rows, width), F32)
    square, product = lax.fori_loop(0, steps, first, (zeros, zeros))
    scale = lax.rsqrt(jnp.sum(square, axis=1, keepdims=True) * (1.0 / inner) + EPSILON)
    pull = scale * scale * scale * (jnp.sum(product, axis=1, keepdims=True) * (1.0 / inner))

    def conv_back(at, proj_at, pre, grad):
        gate = sigmoid(pre)
        grad = grad * (gate * (1.0 + pre * (1.0 - gate)))
        here = pl.ds(at, width)
        conv_in = proj_ref[:, pl.ds(proj_at, width)]
        taps = cw_ref[:, here]
        dcb_ref[:, here] += jnp.sum(grad, axis=0, keepdims=True)
        dcw_ref[0:1, here] += jnp.sum(grad * conv_in, axis=0, keepdims=True)
        back = taps[0:1] * grad
        for lag, keep in enumerate(slot.keeps, 1):
            kept = grad * keep
            dcw_ref[lag : lag + 1, here] += jnp.sum(
                kept * pltpu.roll(conv_in, lag, 0), axis=0, keepdims=True
            )
            back = back + pltpu.roll(taps[lag : lag + 1] * kept, rows - lag, 0)
        dproj_ref[:, pl.ds(proj_at, width)] = back.astype(BF16)

    def second(index, carry):
        d_scores, sums = carry
        at = pl.multiple_of(index * width, width)
        here = pl.ds(at, width)
        gate = proj_ref[:, here]
        opened = sigmoid(gate)
        scanned = scan_ref[:, here]
        gated = scanned * (gate * opened)
        d_norm = dmix_ref[:, here] * slot.valid
        d_gated = scale * (d_norm * gain_ref[:, here]) - gated * pull
        dgain_ref[:, here] += jnp.sum(d_norm * gated * scale, axis=0, keepdims=True)
        d_scan = d_gated * (gate * opened)
        dproj_ref[:, here] = (
            d_gated * scanned * (opened * (1.0 + gate * (1.0 - opened)))
        ).astype(BF16)
        pre = pre_ref[:, here]
        xs = pre * sigmoid(pre)
        dskip_ref[:, here] += jnp.sum(d_scan * xs, axis=0, keepdims=True)
        cum = spread_ref[:rows, here]
        step = spread_ref[rows:, here]
        decay = decay_ref[:, here]
        scaled = slot.diagonal(split(xs * step, 2))
        d_split = split(d_scan, 2)
        d_weights = mm3(d_split, scaled, NT)
        by_decay = d_weights * decay
        d_scores = d_scores + by_decay
        across = jnp.sum(jnp.where(slot.eye, cum, 0.0), axis=0, keepdims=True)
        decay_back = jnp.exp(jnp.where(slot.anti, across - cum, -1e30))
        weights_back = split(scores_back * decay_back, 2)
        d_scaled = mm3(weights_back, slot.diagonal(d_split), NN)
        flow = by_decay * slot.scores
        net = flow - jnp.where(slot.eye, jnp.sum(flow, axis=0, keepdims=True), 0.0)
        both = jnp.concatenate([net, d_scaled * xs], axis=0)
        sums = sums + mm_exact(both, collect_ref[pl.ds(at, width), :], NN, 2)
        grad = d_scaled * step + skip_ref[:, here] * d_scan
        conv_back(at, pl.multiple_of(inner + at, width), pre, grad)
        return d_scores, sums

    d_scores, sums = lax.fori_loop(
        0, steps, second, (zeros, jnp.zeros((2 * rows, slot.heads), F32))
    )
    d_split = split(d_scores, 2)
    d_c = mm3(d_split, slot.b_tall, NN)
    d_b_tall = mm3(d_split, slot.c_split, TN)
    d_b = d_b_tall[:rows]
    for part in range(1, PACK):
        d_b = d_b + d_b_tall[part * rows : (part + 1) * rows]
    conv_back(inner, slot.bc_at, slot.bc_pre, jnp.concatenate([d_b, d_c], axis=1))
    d_decay = mm_exact(slot.triu, sums[:rows], NN)
    d_step = sums[rows:] + d_decay * slot.rate
    dalog_ref[...] += jnp.sum(d_decay * slot.log_decay, axis=0, keepdims=True)
    d_dt = d_step * sigmoid(slot.dt_in)
    ddt_ref[...] += jnp.sum(d_dt, axis=0, keepdims=True)
    dproj_ref[:, inner + conv :] = d_dt.astype(BF16)


def whole(array):
    return pl.BlockSpec(array.shape, lambda slot: (0,) * array.ndim)


def per_slot(rows, columns):
    return pl.BlockSpec((rows, columns), lambda slot: (slot, 0))


def mixer_sizes(projected, fill, params):
    taps, bias, dt_bias, _, _, gain = params
    return (
        projected.shape[0] // fill.shape[0],
        fill.shape[1],
        gain.shape[1],
        bias.shape[1],
        dt_bias.shape[1],
    )


def mixer_forward(projected, fill, link, params, expand):
    sizes = mixer_sizes(projected, fill, params)
    rows, _, inner, _, _ = sizes
    smem = pl.BlockSpec(memory_space=pltpu.SMEM)
    return pl.pallas_call(
        functools.partial(forward_kernel, sizes),
        grid=(fill.shape[0],),
        in_specs=[smem, smem, per_slot(rows, projected.shape[1])]
        + [whole(item) for item in params]
        + [whole(expand)],
        out_specs=per_slot(rows, inner),
        out_shape=jax.ShapeDtypeStruct((projected.shape[0], inner), BF16),
        scratch_shapes=[pltpu.VMEM((2 * rows, inner), F32), pltpu.VMEM((rows, inner), F32)],
        compiler_params=pltpu.CompilerParams(vmem_limit_bytes=VMEM_LIMIT),
        name="mixer_forward",
    )(fill, link, projected, *params, expand)


def mixer_backward(projected, d_mixed, fill, link, params, expand, collect):
    sizes = mixer_sizes(projected, fill, params)
    rows, _, inner, conv, heads = sizes
    smem = pl.BlockSpec(memory_space=pltpu.SMEM)
    taps = params[0].shape[0]
    smalls = [(taps, conv), (1, conv), (1, heads), (1, heads), (1, inner), (1, inner)]
    return pl.pallas_call(
        functools.partial(backward_kernel, sizes),
        grid=(fill.shape[0],),
        in_specs=[smem, smem, per_slot(rows, projected.shape[1]), per_slot(rows, inner)]
        + [whole(item) for item in params]
        + [whole(expand), whole(collect)],
        out_specs=[per_slot(rows, projected.shape[1])]
        + [pl.BlockSpec(shape, lambda slot: (0, 0)) for shape in smalls],
        out_shape=[jax.ShapeDtypeStruct(projected.shape, BF16)]
        + [jax.ShapeDtypeStruct(shape, F32) for shape in smalls],
        scratch_shapes=[pltpu.VMEM((2 * rows, inner), F32)]
        + [pltpu.VMEM((rows, inner), F32)] * 3,
        compiler_params=pltpu.CompilerParams(vmem_limit_bytes=VMEM_LIMIT),
        name="mixer_backward",
    )(fill, link, projected, d_mixed, *params, expand, collect)


def on_device(
    tokens_in,
    out_cotangent,
    in_weight,
    out_weight,
    norm_gain,
    conv_weight,
    conv_bias,
    dt_bias,
    a_log,
    skip_gain,
    gate_gain,
    group_fill,
    group_link,
):
    section_count = lax.axis_size("section")
    section_index = lax.axis_index("section")
    is_first = section_index == 0
    is_last = section_index == section_count - 1
    micro_count, slot_rows, model = tokens_in.shape
    heads, inner = dt_bias.shape[1], gate_gain.shape[1]
    head_size = inner // heads
    expand = jnp.repeat(jnp.eye(heads, dtype=BF16), head_size, axis=1)
    collect = jnp.repeat(jnp.eye(heads, dtype=BF16), head_size, axis=0)
    params = (
        conv_weight[0], conv_bias, dt_bias, a_log, jnp.repeat(skip_gain, head_size, axis=1),
        gate_gain,
    )
    weight_in = lax.all_gather(in_weight[0], "dp", axis=0, tiled=True)
    weight_out = lax.all_gather(out_weight[0], "dp", axis=0, tiled=True)
    own_rows = tokens_in.reshape(-1, model)
    own_grad = out_cotangent.reshape(-1, model)

    layer_in = own_rows
    for step in range(section_count):
        residual = layer_in.astype(F32)
        normed = norm_map(residual, norm_gain).astype(BF16)
        projected = mm(normed, weight_in, NN)
        mixed = mixer_forward(projected, group_fill, group_link, params, expand)
        output = residual + mm(mixed, weight_out, NN)
        if step < section_count - 1:
            received = shifted_2(output.astype(BF16), "section", 1)
            layer_in = jnp.where(is_first, own_rows, received)

    up_low = own_grad
    for step in range(section_count):
        upstream = up_low.astype(F32)
        d_mixed = mm(up_low, weight_out, NT)
        pulled = mixer_backward(
            projected, d_mixed, group_fill, group_link, params, expand, collect
        )
        d_low = pulled[0]
        d_normed = mm(d_low, weight_in, NT)
        _, pull_norm = jax.vjp(norm_map, residual, norm_gain)
        d_residual, d_gain = pull_norm(d_normed)
        input_grad = upstream + d_residual
        if step < section_count - 1:
            received = shifted_2(input_grad.astype(BF16), "section", -1)
            up_low = jnp.where(is_last, own_grad, received)

    shard_out = lax.psum_scatter(
        mm(mixed, up_low, TN).astype(BF16), "dp", scatter_dimension=0, tiled=True
    ).astype(F32)
    shard_in = lax.psum_scatter(
        mm(normed, d_low, TN).astype(BF16), "dp", scatter_dimension=0, tiled=True
    ).astype(F32)
    smalls = (d_gain,) + tuple(pulled[1:])
    flat = jnp.concatenate([item.reshape(-1) for item in smalls])
    flat = lax.psum(flat, "dp")
    summed, at = [], 0
    for item in smalls:
        summed.append(flat[at : at + item.size].reshape(item.shape))
        at += item.size
    gain_sum, taps_sum, bias_sum, dt_sum, alog_sum, skip_sum, gate_sum = summed
    skip_sum = skip_sum.reshape(1, heads, head_size).sum(axis=2)
    shape = (1, micro_count, slot_rows, model)
    return (
        output.reshape(shape),
        input_grad.reshape(shape),
        shard_in[None],
        shard_out[None],
        gain_sum,
        taps_sum[None],
        bias_sum,
        dt_sum,
        alog_sum,
        skip_sum,
        gate_sum,
    )


def solution(mesh):
    in_specs = (
        P(None, "dp", None),
        P(None, "dp", None),
        P("section", "dp", None),
        P("section", "dp", None),
        P("section", None),
        P("section", None, None),
        P("section", None),
        P("section", None),
        P("section", None),
        P("section", None),
        P("section", None),
        P(None, "dp"),
        P(None, "dp"),
    )
    out_specs = (
        P("section", None, "dp", None),
        P("section", None, "dp", None),
        P("section", "dp", None),
        P("section", "dp", None),
        P("section", None),
        P("section", None, None),
        P("section", None),
        P("section", None),
        P("section", None),
        P("section", None),
        P("section", None),
    )
    return jax.shard_map(
        on_device, mesh=mesh, in_specs=in_specs, out_specs=out_specs, check_vma=False
    )
```

time: 1090 us -> 544 us (0.50); the launches traced: 1080 us -> 543 us
  matrix products: 249 us -> 54 us
  local copies, waits for them, and re-layouts: 170 us -> 16 us
  other arithmetic: 161 us -> 8.24 us
  Pallas kernels: 0 us -> 79.5 us
  blocking collectives: 61.2 us -> 0 us
  loops' own time: 39.4 us -> 0 us
  starting transfers between devices: 21.8 us -> 5.07 us
    dot_general x70 -> x10, matrix products: 208 us -> 54 us  [mm(): return lax.dot_general(left, right, dims, preferred_element_type=F32)]
    pallas_call x0 -> x4, Pallas kernels: none -> 79.5 us  [the longest x2 56.2 us: mixer_backward(): pl.pallas_call(functools.partial(backward_kernel, sizes), grid=(fill.shap...]
    psum x0 -> x1, waiting for transfers between devices: none -> 71.5 us  [on_device(): flat = lax.psum(flat, 'dp')]
    psum x1 -> x0, blocking collectives: 61.2 us -> none  [on_device(): summed = lax.psum(small_sums, 'dp')]
    reduce_scatter x2, waiting for transfers between devices: 223 us -> 181 us  [the longest x1 111 us: on_device(): lax.psum_scatter(mm(normed, d_low, TN).astype(BF16), 'dp', scatter_dimens...]
    another operation x2 -> x0, loops' own time: 39.4 us -> none  [the longest x1 33.3 us: on_device(): carry_end, tick_outputs = lax.scan(backward_tick, carry_start, tick_list)]
    mul x36 -> x0, other arithmetic: 34.9 us -> none  [the longest x8 15.4 us: mixer_slot(): activated = jax.nn.silu(conv_sum)]
    reduce_sum x28 -> x1, other arithmetic: 33.8 us -> 0.63 us  [on_device(): skip_sum = skip_sum.reshape(1, heads, head_size).sum(axis=2)]
  transfers between devices with their start and end apart: 12 -> 7, of which waited for: 12 -> 6; matrix products, arithmetic and copies ran while one was open for 4% -> 8% of each run, Pallas kernels for 0% -> 4%
where the time goes in v1:
time: 544 us; the launch traced here: 543 us
  waiting for transfers between devices  366 us (67%)
  Pallas kernels  79.5 us (15%)
  matrix products  54 us (10%)
  local copies, waits for them, and re-layouts  16 us (3%)
  between operations  14 us (3%)
  other arithmetic  8.24 us (2%)
    reduce_scatter x1, waiting for transfers between devices, on_device(): lax.psum_scatter(mm(normed, d_low, TN).astype(BF16), 'dp', scatter_dimens...  111 us
    all_gather x1, waiting for transfers between devices, on_device(): weight_in = lax.all_gather(in_weight[0], 'dp', axis=0, tiled=True)  77.1 us
    psum x1, waiting for transfers between devices, on_device(): flat = lax.psum(flat, 'dp')  71.5 us
    reduce_scatter x1, waiting for transfers between devices, on_device(): lax.psum_scatter(mm(mixed, up_low, TN).astype(BF16), 'dp', scatter_dimens...  69.9 us
    pallas_call x2, Pallas kernels, mixer_backward(): pl.pallas_call(functools.partial(backward_kernel, sizes), grid=(fill.shap...  56.2 us
    dot_general x10, matrix products, mm(): return lax.dot_general(left, right, dims, preferred_element_type=F32)  54 us
    all_gather x1, waiting for transfers between devices, on_device(): weight_out = lax.all_gather(out_weight[0], 'dp', axis=0, tiled=True)  31.9 us
    pallas_call x2, Pallas kernels, mixer_forward(): pl.pallas_call(functools.partial(forward_kernel, sizes), grid=(fill.shape...  23.2 us
  transfers between devices with their start and end apart: 7, of which 6 were waited for; matrix products, arithmetic and copies ran while one was open for 8% of the time, Pallas kernels for 4%

profile of v1, /device:TPU:0, one launch (start us, length us, event | category | flops | bytes accessed | tf_op | source)
XLA Modules:
  0.0 543.1 jit_solution(1368081581373072126)
XLA Ops:
  8.7 1.3 copy.32.fill_ref
  10.0 1.3 copy.33.link_ref
  11.4 1.1 multiply_reduce_fusion
  15.2 77.1 %all-gather.5.cloned.1.call-done = bf16[1,1024,4384]{2,1,0:T(8,128)(2,1)} async-done(((bf16[1,64,4384]{2,1,0:T(8,128)(2,1)}), bf16[1,1024,4384]{2,1,0:T(8,128)(2,1)}) %all-gather.5.cloned.1.call-update) | async-done | bytes 8978448 | tf_op jit(solution)/shard_map/all_gather | solution.py:377
  92.3 7.5 %fusion.6.proj_ref = f32[192,4384]{1,0:T(8,128)} fusion(bf16[1,1024,4384]{2,1,0:T(8,128)(2,1)} %all-gather.5.cloned.1.call-done, bf16[192,1024]{1,0:T(8,128)(2,1)} %bitcast.69, f32[1024]{0:T(1024)} %bitcast.74, f32[192]{0:T(256)S(1)} %rsqrt.26), kind=kOutput, calls=%fused_computation.7 | convolution fusion | flops 1724645376 | bytes 12743424 | tf_op jit(solution)/shard_map/dot_general | solution.py:33
  99.8 11.6 %mixer_forward.2 = bf16[192,2048]{1,0:T(8,128)(2,1)} custom-call(s32[3,2]{1,0:T(4,128)} %copy.32.fill_ref, s32[3,2]{1,0:T(4,128)} %copy.33.link_ref, f32[192,4384]{1,0:T(8,128)} %fusion.6.proj_ref, f32[4,2304]{1,0:T(4,128)} %bitcast.80, f32[1,2304]{1,0:T(1,128)} %cb_ref.7, f32[1,32]{1,0:T(1,128)} %dtb_ref.7, f32[1,32]{1,0:T(1,128)} %alog_ref.7, ...), custom_call_target="tpu_custom_call" | custom-call | tf_op jit(solution)/shard_map/mixer_forward/pallas_call | solution.py:312
  111.4 31.9 %all-gather.7.cloned.1.call-done = bf16[1,2048,1024]{2,1,0:T(8,128)(2,1)} async-done(((bf16[1,128,1024]{2,1,0:T(8,128)(2,1)}), bf16[1,2048,1024]{2,1,0:T(8,128)(2,1)}) %all-gather.7.cloned.1.call-update) | async-done | bytes 4194320 | tf_op jit(solution)/shard_map/all_gather | solution.py:378
  143.3 3.4 fusion.24
  146.8 3.4 collective-permute-start
  150.2 4.9 fusion.10.dmix_ref
  155.1 3.9 collective-permute-done
  159.2 7.4 %fusion.4.proj_ref = f32[192,4384]{1,0:T(8,128)} fusion(bf16[1,1024,4384]{2,1,0:T(8,128)(2,1)} %all-gather.5.cloned.1.call-done, bf16[192,1024]{1,0:T(8,128)(2,1)S(1)} %broadcast_select_fusion.1, f32[192]{0:T(256)S(1)} %fusion.45, f32[1024]{0:T(1024)S(1)} %bitcast.75), kind=kOutput, calls=%fused_computation.5 | convolution fusion | flops 1724645376 | bytes 12743424 | tf_op jit(solution)/shard_map/dot_general | solution.py:33
  167.5 28.1 %mixer_backward.2 = (bf16[192,4384]{1,0:T(8,128)(2,1)}, f32[4,2304]{1,0:T(4,128)}, f32[1,2304]{1,0:T(1,128)}, f32[1,32]{1,0:T(1,128)}, f32[1,32]{1,0:T(1,128)}, /*index=5*/f32[1,2048]{1,0:T(1,128)}, f32[1,2048]{1,0:T(1,128)}) custom-call(s32[3,2]{1,0:T(4,128)} %copy.32.fill_ref, s32[3,2]{1,0:T(4,128)} %copy.33.link_ref, f32[192,4384]{1,0:T(8,128)} %fusion.4.proj_ref, ...), custom_call_target="tpu_custom_call" | custom-call | tf_op jit(solution)/shard_map/mixer_backward/pallas_call | solution.py:332
  195.6 7.4 %fusion.37 = (f32[192]{0:T(256)S(1)}, f32[192,1024]{1,0:T(8,128)S(1)}) fusion(bf16[192,1024]{1,0:T(8,128)(2,1)S(1)} %broadcast_select_fusion.1, f32[1024]{0:T(1024)S(1)} %bitcast.76, bf16[192,4384]{1,0:T(8,128)(2,1)} %get-tuple-element.19, bf16[1,1024,4384]{2,1,0:T(8,128)(2,1)} %all-gather.5.cloned.1.call-done), kind=kOutput, calls=%fused_computation.41 | convolution fusion | flops 1724645120 | bytes 11846400 | tf_op jit(solution)/shard_map/dot_general | solution.py:33
  203.3 1.5 collective-permute-start.1
  204.8 11.6 %mixer_forward.3 = bf16[192,2048]{1,0:T(8,128)(2,1)} custom-call(s32[3,2]{1,0:T(4,128)} %copy.32.fill_ref, s32[3,2]{1,0:T(4,128)} %copy.33.link_ref, f32[192,4384]{1,0:T(8,128)} %fusion.4.proj_ref, f32[4,2304]{1,0:T(4,128)} %bitcast.82, f32[1,2304]{1,0:T(1,128)} %cb_ref.7, f32[1,32]{1,0:T(1,128)} %dtb_ref.7, f32[1,32]{1,0:T(1,128)} %alog_ref.7, ...), custom_call_target="tpu_custom_call" | custom-call | tf_op jit(solution)/shard_map/mixer_forward/pallas_call | solution.py:312
  216.5 2.7 fusion.8.dmix_ref
  219.2 28.1 %mixer_backward.3 = (bf16[192,4384]{1,0:T(8,128)(2,1)}, f32[4,2304]{1,0:T(4,128)}, f32[1,2304]{1,0:T(1,128)}, f32[1,32]{1,0:T(1,128)}, f32[1,32]{1,0:T(1,128)}, /*index=5*/f32[1,2048]{1,0:T(1,128)}, f32[1,2048]{1,0:T(1,128)}) custom-call(s32[3,2]{1,0:T(4,128)} %copy.32.fill_ref, s32[3,2]{1,0:T(4,128)} %copy.33.link_ref, f32[192,4384]{1,0:T(8,128)} %fusion.4.proj_ref, ...), custom_call_target="tpu_custom_call" | custom-call | tf_op jit(solution)/shard_map/mixer_backward/pallas_call | solution.py:332
  248.9 8.2 %fusion.30 = (f32[1024]{0:T(1024)S(1)}, f32[192]{0:T(256)S(1)}, f32[192,1024]{1,0:T(8,128)}) fusion(bf16[192,1024]{1,0:T(8,128)(2,1)S(1)} %broadcast_select_fusion.1, f32[192]{0:T(256)S(1)} %fusion.45, f32[1024]{0:T(1024)S(1)} %bitcast.77, bf16[192,4384]{1,0:T(8,128)(2,1)} %get-tuple-element.20, bf16[1,1024,4384]{2,1,0:T(8,128)(2,1)} %all-gather.5.cloned.1.call-done), kind=kOutput, calls=%fused_computation.34 | convolution fusion | flops 1725233920 | bytes 11851264 | tf_op jit(solution)/shard_map/dot_general | solution.py:33
  257.9 3.3 convolution_convert_fusion.1
  261.3 1.4 copy-done.4
  262.7 5.1 convolution_convert_fusion
  267.8 4.2 convert_add_fusion
  272.0 1.2 fusion.35
  273.1 71.5 %all-reduce.2.cloned.1.call-done = f32[16704]{0:T(1024)} async-done(((f32[16704]{0:T(1024)}), f32[16704]{0:T(1024)}) %all-reduce.2.cloned.1.call-update) | async-done | bytes 66832 | tf_op jit(solution)/shard_map/psum | solution.py:417
  347.3 1.5 fusion.46
  349.4 1.3 slice.34
  350.7 1.3 slice_bitcast_fusion
  352.1 69.9 %reduce-scatter.5.cloned.1.call-done = bf16[128,1024]{1,0:T(8,128)(2,1)} async-done(((bf16[2048,1024]{1,0:T(8,128)(2,1)}), bf16[128,1024]{1,0:T(8,128)(2,1)}) %reduce-scatter.5.cloned.1.call-update) | async-done | bytes 262160 | tf_op jit(solution)/shard_map/reduce_scatter | solution.py:409
  422.0 1.8 bitcast_convert_fusion.1
  423.8 110.7 %reduce-scatter.3.cloned.1.call-done = bf16[64,4384]{1,0:T(8,128)(2,1)} async-done(((bf16[1024,4384]{1,0:T(8,128)(2,1)}), bf16[64,4384]{1,0:T(8,128)(2,1)}) %reduce-scatter.3.cloned.1.call-update) | async-done | bytes 561168 | tf_op jit(solution)/shard_map/reduce_scatter | solution.py:412
  534.5 2.1 bitcast_convert_fusion
  (56 shorter events, 11.5 us)
Async XLA Ops:
  7.2 85.1 %all-gather.5.cloned.1.call-start = ((), (), s32[]{:S(2)}) async-start(), calls=%async_computation.5 | async-start | bytes 9748480 | tf_op jit(solution)/shard_map/all_gather | solution.py:377
  7.9 135.4 %all-gather.7.cloned.1.call-start = ((), (), s32[]{:S(2)}) async-start(), calls=%async_computation.6 | async-start | bytes 4456448 | tf_op jit(solution)/shard_map/all_gather | solution.py:378
  8.7 335.9 %all-reduce.2.cloned.1.call-start = ((), (), s32[]{:S(2)}) async-start(), calls=%async_computation.4 | async-start | bytes 139264 | tf_op jit(solution)/shard_map/psum | solution.py:417
  99.8 43.5 %copy-start.2 = (bf16[3,64,1024]{2,1,0:T(8,128)(2,1)S(1)}, bf16[3,64,1024]{2,1,0:T(8,128)(2,1)}, u32[]{:S(2)}) copy-start(bf16[3,64,1024]{2,1,0:T(8,128)(2,1)} %param.13) | copy-start | bytes 1179652
  99.8 50.4 %copy-start.3 = (bf16[3,64,1024]{2,1,0:T(8,128)(2,1)S(1)}, bf16[3,64,1024]{2,1,0:T(8,128)(2,1)}, u32[]{:S(2)}) copy-start(bf16[3,64,1024]{2,1,0:T(8,128)(2,1)} %param.14) | copy-start | bytes 1179652
  146.8 12.4 %copy-start.6 = (f32[1,1024]{1,0:T(1,128)S(1)}, f32[1,1024]{1,0:T(1,128)}, u32[]{:S(2)}) copy-start(f32[1,1024]{1,0:T(1,128)} %param.17) | copy-start | bytes 12292
  146.8 12.1 %collective-permute-start = (bf16[192,1024]{1,0:T(8,128)(2,1)S(1)}, bf16[192,1024]{1,0:T(8,128)(2,1)S(1)}, u32[]{:S(2)}, u32[]{:S(2)}) collective-permute-start(bf16[192,1024]{1,0:T(8,128)(2,1)S(1)} %fusion.24), channel_id=1, source_target_pairs={{0,16},{1,17},{2,18},{3,19},{4,20},{5,21},{6,22},{7,23},{8,24},{9,... | collective-permute-start | bytes 1179656 | tf_op jit(solution)/shard_map/ppermute | solution.py:23
  203.3 13.1 %collective-permute-start.1 = (bf16[192,1024]{1,0:T(8,128)(2,1)S(1)}, bf16[192,1024]{1,0:T(8,128)(2,1)S(1)}, u32[]{:S(2)}, u32[]{:S(2)}) collective-permute-start(bf16[192,1024]{1,0:T(8,128)(2,1)S(1)} %fusion.34), channel_id=1, source_target_pairs={{16,0},{17,1},{18,2},{19,3},{20,4},{21,5},{22,6},{23,7},{24,8},{25... | collective-permute-start | bytes 1179656 | tf_op jit(solution)/shard_map/ppermute | solution.py:23
  204.8 11.7 %copy-start = (bf16[1,2048,1024]{2,1,0:T(8,128)(2,1)S(1)}, bf16[1,2048,1024]{2,1,0:T(8,128)(2,1)}, u32[]{:S(2)}) copy-start(bf16[1,2048,1024]{2,1,0:T(8,128)(2,1)} %all-gather.7.cloned.1.call-done) | copy-start | bytes 12582916
  248.8 8.3 %copy-start.7 = (f32[1,2048]{1,0:T(1,128)S(1)}, f32[1,2048]{1,0:T(1,128)}, u32[]{:S(2)}) copy-start(f32[1,2048]{1,0:T(1,128)} %get-tuple-element.25) | copy-start | bytes 24580
  248.8 8.3 %copy-start.8 = (f32[1,2048]{1,0:T(1,128)S(1)}, f32[1,2048]{1,0:T(1,128)}, u32[]{:S(2)}) copy-start(f32[1,2048]{1,0:T(1,128)} %get-tuple-element.26) | copy-start | bytes 24580
  248.9 8.3 %copy-start.9 = (f32[1,32]{1,0:T(1,128)S(1)}, f32[1,32]{1,0:T(1,128)}, u32[]{:S(2)}) copy-start(f32[1,32]{1,0:T(1,128)} %get-tuple-element.23) | copy-start | bytes 388
  248.9 8.3 %copy-start.10 = (f32[1,32]{1,0:T(1,128)S(1)}, f32[1,32]{1,0:T(1,128)}, u32[]{:S(2)}) copy-start(f32[1,32]{1,0:T(1,128)} %get-tuple-element.24) | copy-start | bytes 388
  248.9 9.0 %copy-start.1 = (bf16[192,2048]{1,0:T(8,128)(2,1)S(1)}, bf16[192,2048]{1,0:T(8,128)(2,1)}, u32[]{:S(2)}) copy-start(bf16[192,2048]{1,0:T(8,128)(2,1)} %mixer_forward.3) | copy-start | bytes 2359300
  257.9 164.1 %reduce-scatter.5.cloned.1.call-start = ((), (), s32[]{:S(2)}) async-start(), calls=%async_computation.3 | async-start | bytes 4456448 | tf_op jit(solution)/shard_map/reduce_scatter | solution.py:409
  261.2 1.5 copy-start.4
  261.2 273.2 %reduce-scatter.3.cloned.1.call-start = ((), (), s32[]{:S(2)}) async-start(), calls=%async_computation.2 | async-start | bytes 9748480 | tf_op jit(solution)/shard_map/reduce_scatter | solution.py:412
  267.8 4.2 copy-start.5
Sparse Core Ops, SparseCore 0:
  10.3 81.9 all-gather.4
  94.4 48.8 all-gather.6
  258.0 86.5 all-reduce.1
  348.3 73.6 reduce-scatter.4
  426.0 108.4 reduce-scatter.2
